TPU v7x, 32 devices: a whole 2x2x4 slice. The times are simulated.
32 devices in a mesh: replica: 4 (over x, core), fsdp: 8 (over z, y).
Axes of the slice: x: 2, y: 2, z: 4, core: 2. Of those that a mesh axis runs over, the one named last changes fastest.
Arguments:
- tokens: bfloat16 [32768, 768], P(('replica', 'fsdp')), may hold values from -6 to 6
- lengths: int32 [32], P(('replica', 'fsdp')), may hold values from 513 to 1024, as said below
- random_blocks: int32 [32, 16, 3], P(('replica', 'fsdp')), may hold values from 0 to 15, as said below
- qkv_weight: bfloat16 [768, 2304], P('fsdp'), may hold values from -0.21875 to 0.21875
- out_weight: bfloat16 [768, 768], P('fsdp'), may hold values from -1.75 to 1.75
- up_weight: bfloat16 [768, 3072], P('fsdp'), may hold values from -0.21875 to 0.21875
- down_weight: bfloat16 [3072, 768], P('fsdp'), may hold values from -0.109375 to 0.109375
- proj_bias: bfloat16 [4, 768], P(None, 'fsdp'), may hold values from -3 to 3
- up_bias: bfloat16 [3072], P('fsdp'), may hold values from -3 to 3
- norm_gain: bfloat16 [2, 768], P(None, 'fsdp'), may hold values from 0.5 to 1.5
- norm_bias: bfloat16 [2, 768], P(None, 'fsdp'), may hold values from -3 to 3
- cotangent: bfloat16 [32768, 768], P(('replica', 'fsdp')), may hold values from -6 to 6
Outputs:
- out: bfloat16 [32768, 768], P(('replica', 'fsdp'))
- input_grad: float32 [32768, 768], P(('replica', 'fsdp'))
- qkv_grad: float32 [768, 2304], P('fsdp')
- out_weight_grad: float32 [768, 768], P('fsdp')
- up_grad: float32 [768, 3072], P('fsdp')
- down_grad: float32 [3072, 768], P('fsdp')
- proj_bias_grad: float32 [4, 768], P(None, 'fsdp')
- up_bias_grad: float32 [3072], P('fsdp')
- gain_grad: float32 [2, 768], P(None, 'fsdp')
- norm_bias_grad: float32 [2, 768], P(None, 'fsdp')
Inputs may be any that keep to these rules, and one draw needn't show every extreme that they name: Slot s holds one sequence of lengths[s] positions from its start; the rest is padding. Each entry of random_blocks[s] is below ceil(lengths[s] / 64), so random blocks lie inside the sequence.
All inputs are finite; a program needn't handle non-finite values.
Results may differ from a plain program's by a relative error of at most 0.017.
Values may be sent and summed in bfloat16 or wider, within the bound.
No kernel may reach another device: no remote copies, remote signals or barrier semaphores. Data moves between devices by JAX's collectives and lax.ppermute only.
A program may use at most 256 MiB of HBM per device.

v0:
```python
import math
import jax
import jax.numpy as jnp
from jax import lax
from jax.sharding import PartitionSpec as P

D = 768
H = 12
HD = 64
BLK = 64
norm_eps = 1e-06


def as_sent(array):
    return jax.tree.map(lambda a: a.astype(jnp.bfloat16) if a.dtype == jnp.float32 else a, array)


def layer_norm(hidden, factor, offset):
    centre = hidden - jnp.mean(hidden, axis=-1, keepdims=True)
    variance = jnp.mean(centre * centre, axis=-1, keepdims=True)
    return centre * lax.rsqrt(variance + norm_eps) * factor + offset


def gelu_tanh(values):
    return jax.nn.gelu(values, approximate=True)


def block_mask(length, chosen, seq_len, block_size):
    block_count = chosen.shape[0]
    blocks_used = (length + block_size - 1) // block_size
    query_block = jnp.arange(block_count, dtype=jnp.int32)[:, None]
    key_block = jnp.arange(block_count, dtype=jnp.int32)[None, :]
    nearby = jnp.abs(query_block - key_block) <= 1
    global_key = (key_block == 0) | (key_block == blocks_used - 1)
    global_query = (query_block == 0) | (query_block == blocks_used - 1)
    picked = jnp.any(chosen[:, None, :] == key_block[:, :, None], axis=2)
    allowed = (nearby | global_key | global_query | picked) & (key_block < blocks_used)
    spread_mask = jnp.repeat(jnp.repeat(allowed, block_size, axis=0), block_size, axis=1)
    key_pos = jnp.arange(seq_len, dtype=jnp.int32)[None, :]
    return spread_mask & (key_pos < length)


def masked_scores(query_block, mask_block, keys, scale):
    scores = (
        jnp.einsum("qhd,khd->hqk", query_block, keys, preferred_element_type=jnp.float32) * scale
    )
    return jnp.where(mask_block[None], scores, -1000000000.0)


def forward_block(query_block, mask_block, keys, values, scale):
    scores = masked_scores(query_block, mask_block, keys, scale)
    peak = jnp.max(scores, axis=-1, keepdims=True)
    weights = jnp.exp(scores - peak)
    total = jnp.sum(weights, axis=-1, keepdims=True)
    probs = (weights / total).astype(jnp.bfloat16)
    context = jnp.einsum("hqk,khd->qhd", probs, values, preferred_element_type=jnp.float32)
    return (context, peak + jnp.log(total))


def backward_block(query_block, mask_block, grad_block, logsum, keys, values, scale):
    scores = masked_scores(query_block, mask_block, keys, scale)
    probs = jnp.exp(scores - logsum)
    grad_probs = jnp.einsum("qhd,khd->hqk", grad_block, values, preferred_element_type=jnp.float32)
    inner = jnp.sum(grad_probs * probs, axis=-1, keepdims=True)
    grad_scores = (probs * (grad_probs - inner)).astype(jnp.bfloat16)
    grad_query = (
        jnp.einsum("hqk,khd->qhd", grad_scores, keys, preferred_element_type=jnp.float32) * scale
    )
    grad_key = (
        jnp.einsum("hqk,qhd->khd", grad_scores, query_block, preferred_element_type=jnp.float32)
        * scale
    )
    grad_value = jnp.einsum(
        "hqk,qhd->khd", probs.astype(jnp.bfloat16), grad_block, preferred_element_type=jnp.float32
    )
    return (grad_query, grad_key, grad_value)


def shards(
    tokens,
    lengths,
    random_blocks,
    qkv_weight,
    out_weight,
    up_weight,
    down_weight,
    proj_bias,
    up_bias,
    norm_gain,
    norm_bias,
    cotangent,
):
    seq_len = tokens.shape[0]
    length = lengths[0]
    valid = (jnp.arange(seq_len, dtype=jnp.int32) < length).astype(jnp.float32)[:, None]
    allowed = block_mask(length, random_blocks[0], seq_len, BLK)
    scale = 1.0 / math.sqrt(HD)
    rows_step = min(512, seq_len)
    gathered = (
        lax.all_gather(qkv_weight, "fsdp", axis=0, tiled=True),
        lax.all_gather(out_weight, "fsdp", axis=0, tiled=True),
        lax.all_gather(up_weight, "fsdp", axis=0, tiled=True),
        lax.all_gather(down_weight, "fsdp", axis=0, tiled=True),
        lax.all_gather(proj_bias, "fsdp", axis=1, tiled=True),
        lax.all_gather(up_bias, "fsdp", axis=0, tiled=True),
        lax.all_gather(norm_gain, "fsdp", axis=1, tiled=True),
        lax.all_gather(norm_bias, "fsdp", axis=1, tiled=True),
    )
    qkv_full, out_full, bias_full = (gathered[0], gathered[1], gathered[4])
    early_mlp = (gathered[2], gathered[3], gathered[5], gathered[6], gathered[7])
    mixed = jnp.dot(tokens, qkv_full, preferred_element_type=jnp.float32)
    queries = (mixed[:, :D] + bias_full[0]).astype(jnp.bfloat16).reshape(seq_len, H, HD)
    keys = mixed[:, D : 2 * D].astype(jnp.bfloat16).reshape(seq_len, H, HD)
    values = (mixed[:, 2 * D :] + bias_full[1]).astype(jnp.bfloat16).reshape(seq_len, H, HD)
    contexts = []
    logsums = []
    for begin_row in range(0, seq_len, rows_step):
        context, logsum = forward_block(
            queries[begin_row : begin_row + rows_step],
            allowed[begin_row : begin_row + rows_step],
            keys,
            values,
            scale,
        )
        contexts.append(context)
        logsums.append(logsum)
    context_low = jnp.concatenate(contexts, axis=0).reshape(seq_len, D).astype(jnp.bfloat16)
    branch = jnp.dot(context_low, out_full, preferred_element_type=jnp.float32) + bias_full[2]
    up_full, down_full, up_bias_full, gain_full, shift_full = early_mlp
    gain_float = gain_full.astype(jnp.float32)
    shift_float = shift_full.astype(jnp.float32)
    hidden_one = tokens.astype(jnp.float32) + branch
    normed, first_pull = jax.vjp(layer_norm, hidden_one, gain_float[0], shift_float[0])
    normed_low = normed.astype(jnp.bfloat16)
    upward = jnp.dot(normed_low, up_full, preferred_element_type=jnp.float32) + up_bias_full
    activated, gelu_pull = jax.vjp(gelu_tanh, upward)
    activated_low = activated.astype(jnp.bfloat16)
    downward = jnp.dot(activated_low, down_full, preferred_element_type=jnp.float32) + bias_full[3]
    final_norm, second_pull = jax.vjp(layer_norm, normed + downward, gain_float[1], shift_float[1])
    result = (final_norm * valid).astype(jnp.bfloat16)
    qkv_back, out_back, up_back, down_back = (
        lax.all_gather(qkv_weight, "fsdp", axis=0, tiled=True),
        lax.all_gather(out_weight, "fsdp", axis=0, tiled=True),
        lax.all_gather(up_weight, "fsdp", axis=0, tiled=True),
        lax.all_gather(down_weight, "fsdp", axis=0, tiled=True),
    )
    grad_out = cotangent.astype(jnp.float32) * valid
    grad_two, gain_two, shift_two = second_pull(grad_out)
    grad_down = grad_two.astype(jnp.bfloat16)
    down_grad = jnp.einsum(
        "sf,sd->fd", activated_low, grad_down, preferred_element_type=jnp.float32
    )
    grad_act = jnp.einsum("sd,fd->sf", grad_down, down_back, preferred_element_type=jnp.float32)
    grad_up = gelu_pull(grad_act)[0].astype(jnp.bfloat16)
    up_grad = jnp.einsum("sd,sf->df", normed_low, grad_up, preferred_element_type=jnp.float32)
    up_bias_grad = jnp.sum(grad_up, axis=0, dtype=jnp.float32)
    grad_normed = grad_two + jnp.einsum(
        "sf,df->sd", grad_up, up_back, preferred_element_type=jnp.float32
    )
    grad_one, gain_one, shift_one = first_pull(grad_normed)
    grad_branch = grad_one.astype(jnp.bfloat16)
    out_grad = jnp.einsum("sd,se->de", context_low, grad_branch, preferred_element_type=jnp.float32)
    grad_context = (
        jnp.einsum("se,de->sd", grad_branch, out_back, preferred_element_type=jnp.float32)
        .astype(jnp.bfloat16)
        .reshape(seq_len, H, HD)
    )
    query_parts = []
    key_total = jnp.zeros((seq_len, H, HD), jnp.float32)
    value_total = jnp.zeros((seq_len, H, HD), jnp.float32)
    for block_index, begin_row in enumerate(range(0, seq_len, rows_step)):
        grad_query, grad_key, grad_value = backward_block(
            queries[begin_row : begin_row + rows_step],
            allowed[begin_row : begin_row + rows_step],
            grad_context[begin_row : begin_row + rows_step],
            logsums[block_index],
            keys,
            values,
            scale,
        )
        query_parts.append(grad_query)
        key_total = key_total + grad_key
        value_total = value_total + grad_value
    grad_queries = jnp.concatenate(query_parts, axis=0).reshape(seq_len, D).astype(jnp.bfloat16)
    grad_keys = key_total.reshape(seq_len, D).astype(jnp.bfloat16)
    grad_values = value_total.reshape(seq_len, D).astype(jnp.bfloat16)
    grad_mixed = jnp.concatenate([grad_queries, grad_keys, grad_values], axis=1)
    qkv_grad = jnp.einsum("sd,se->de", tokens, grad_mixed, preferred_element_type=jnp.float32)
    input_grad = grad_one + jnp.einsum(
        "se,de->sd", grad_mixed, qkv_back, preferred_element_type=jnp.float32
    )
    bias_grads = jnp.stack(
        [
            jnp.sum(grad_queries, axis=0, dtype=jnp.float32),
            jnp.sum(grad_values, axis=0, dtype=jnp.float32),
            jnp.sum(grad_branch, axis=0, dtype=jnp.float32),
            jnp.sum(grad_down, axis=0, dtype=jnp.float32),
        ]
    )
    gain_grads = jnp.stack([gain_one, gain_two])
    shift_grads = jnp.stack([shift_one, shift_two])
    shares = (
        lax.psum_scatter(qkv_grad, "fsdp", scatter_dimension=0, tiled=True),
        lax.psum_scatter(out_grad, "fsdp", scatter_dimension=0, tiled=True),
        lax.psum_scatter(up_grad, "fsdp", scatter_dimension=0, tiled=True),
        lax.psum_scatter(down_grad, "fsdp", scatter_dimension=0, tiled=True),
        lax.psum_scatter(bias_grads, "fsdp", scatter_dimension=1, tiled=True),
        lax.psum_scatter(up_bias_grad, "fsdp", scatter_dimension=0, tiled=True),
        lax.psum_scatter(gain_grads, "fsdp", scatter_dimension=1, tiled=True),
        lax.psum_scatter(shift_grads, "fsdp", scatter_dimension=1, tiled=True),
    )
    totals = jax.tree.map(
        lambda part: part.astype(jnp.float32), lax.psum(as_sent(tuple(shares)), "replica")
    )
    return (
        result,
        input_grad,
        totals[0],
        totals[1],
        totals[2],
        totals[3],
        totals[4],
        totals[5],
        totals[6],
        totals[7],
    )


def solution(mesh):
    return jax.shard_map(
        shards,
        mesh=mesh,
        in_specs=(
            P(("replica", "fsdp"), None),
            P(("replica", "fsdp")),
            P(("replica", "fsdp"), None, None),
            P("fsdp", None),
            P("fsdp", None),
            P("fsdp", None),
            P("fsdp", None),
            P(None, "fsdp"),
            P("fsdp"),
            P(None, "fsdp"),
            P(None, "fsdp"),
            P(("replica", "fsdp"), None),
        ),
        out_specs=(
            P(("replica", "fsdp"), None),
            P(("replica", "fsdp"), None),
            P("fsdp", None),
            P("fsdp", None),
            P("fsdp", None),
            P("fsdp", None),
            P(None, "fsdp"),
            P("fsdp"),
            P(None, "fsdp"),
            P(None, "fsdp"),
        ),
        check_vma=False,
    )
```

profile of v0, /device:TPU:0, one launch (start us, length us, event | category | flops | bytes accessed | tf_op | source)
XLA Modules:
  0.0 1199.1 jit_solution(17224826126633601862)
XLA Ops:
  12.9 22.3 %all-gather.1 = bf16[8,96,2]{1,2,0:T(2,128)(2,1)S(1)} all-gather(bf16[1,96,2]{1,2,0:T(2,128)(2,1)} %bitcast.138), channel_id=1, replica_groups=mesh['replica'=4,'fsdp'=8] {'fsdp'}, dimensions={0}, use_global_device_ids=true | all-gather | bytes 3456 | tf_op jit(solution)/shard_map/all_gather | solution.py:106
  35.3 16.4 %all-gather.2 = bf16[8,96,2]{1,2,0:T(2,128)(2,1)S(1)} all-gather(bf16[1,96,2]{1,2,0:T(2,128)(2,1)} %bitcast.139), channel_id=1, replica_groups=mesh['replica'=4,'fsdp'=8] {'fsdp'}, dimensions={0}, use_global_device_ids=true | all-gather | bytes 3456 | tf_op jit(solution)/shard_map/all_gather | solution.py:107
  51.9 18.6 %all-gather = bf16[8,96,4]{1,2,0:T(4,128)(2,1)S(1)} all-gather(bf16[1,96,4]{1,2,0:T(4,128)(2,1)} %bitcast.137), channel_id=1, replica_groups=mesh['replica'=4,'fsdp'=8] {'fsdp'}, dimensions={0}, use_global_device_ids=true | all-gather | bytes 6912 | tf_op jit(solution)/shard_map/all_gather | solution.py:104
  71.2 25.9 %all-gather.3 = bf16[8,1,384]{2,1,0:T(2,128)(2,1)S(1)} all-gather(bf16[1,1,384]{2,1,0:T(2,128)(2,1)S(1)} %reshape.199), channel_id=1, replica_groups=mesh['replica'=4,'fsdp'=8] {'fsdp'}, dimensions={0}, use_global_device_ids=true | all-gather | bytes 6912 | tf_op jit(solution)/shard_map/all_gather | solution.py:105
  126.5 12.6 %fusion.20 = (f32[12,512]{1,0:T(8,128)S(1)}, f32[12,512,1024]{2,1,0:T(8,128)}) fusion(pred[512,1024]{1,0:T(8,128)(4,1)} %copy.100, bf16[512,12,64]{0,2,1:T(8,128)(2,1)} %bitcast.108, bf16[1024,12,64]{0,2,1:T(8,128)(2,1)S(1)} %bitcast.100), kind=kOutput, calls=%fused_computation.34 | convolution fusion | flops 824174592 | bytes 28073984 | tf_op jit(solution)/shard_map/qhd,khd->hqk/dot_general | solution.py:45
  139.2 12.4 %fusion.1 = f32[12,512]{1,0:T(8,128)S(1)} fusion(f32[12,512]{1,0:T(8,128)S(1)} %get-tuple-element.103, f32[12,512,1024]{2,1,0:T(8,128)} %get-tuple-element.104, pred[512,1024]{1,0:T(8,128)(4,1)S(1)} %copy-done.13), kind=kLoop, calls=%fused_computation.13 | loop fusion | flops 25159680 | bytes 25739264 | tf_op jit(solution)/shard_map/reduce_sum | solution.py:54
  154.7 8.4 fusion.32
  163.1 12.2 %fusion.19 = (f32[12,512]{1,0:T(8,128)S(1)}, f32[12,512,1024]{2,1,0:T(8,128)}) fusion(pred[512,1024]{1,0:T(8,128)(4,1)S(1)} %copy-done.10, bf16[512,12,64]{0,2,1:T(8,128)(2,1)} %bitcast.110, bf16[1024,12,64]{0,2,1:T(8,128)(2,1)S(1)} %bitcast.101), kind=kOutput, calls=%fused_computation.33 | convolution fusion | flops 824174592 | bytes 28073984 | tf_op jit(solution)/shard_map/qhd,khd->hqk/dot_general | solution.py:45
  175.3 12.4 %fusion = f32[12,512]{1,0:T(8,128)S(1)} fusion(f32[12,512]{1,0:T(8,128)S(1)} %get-tuple-element.105, f32[12,512,1024]{2,1,0:T(8,128)} %get-tuple-element.106, pred[512,1024]{1,0:T(8,128)(4,1)S(1)} %copy-done.10), kind=kLoop, calls=%fused_computation.12 | loop fusion | flops 25159680 | bytes 25739264 | tf_op jit(solution)/shard_map/reduce_sum | solution.py:54
  204.4 11.2 fusion.57
  215.6 65.6 %all-gather.15.cloned.1.call-done = bf16[3072,768]{1,0:T(8,128)(2,1)} async-done(((bf16[384,768]{1,0:T(8,128)(2,1)}), bf16[3072,768]{1,0:T(8,128)(2,1)}) %all-gather.15.cloned.1.call-update) | async-done | bytes 4718608 | tf_op jit(solution)/shard_map/all_gather | solution.py:103
  281.2 11.7 fusion.66
  300.4 18.1 %convert_reduce_fusion = (f32[3072]{0:T(1024)}, bf16[1024,3072]{1,0:T(8,128)(2,1)}) fusion(f32[1024,3072]{1,0:T(8,128)} %fusion.57, f32[3072]{0:T(1024)S(1)} %bitcast.134, bf16[1024,768]{0,1:T(8,128)(2,1)S(1)} %get-tuple-element.89, bf16[3072,768]{1,0:T(8,128)(2,1)} %all-gather.15.cloned.1.call-done), kind=kOutput, calls=%fused_computation.27 | convolution fusion | flops 4904186880 | bytes 25190400 | tf_op jit(solution)/shard_map/sd,fd->sf/dot_general | solution.py:153
  318.4 9.8 multiply_reduce_fusion.3
  337.7 21.3 %multiply_reduce_fusion.1 = (f32[12,512]{1,0:T(8,128)S(1)}, f32[12,512,1024]{2,1,0:T(8,128)}) fusion(f32[12,512]{1,0:T(8,128)S(1)} %log_add_fusion.1, f32[12,512,1024]{2,1,0:T(8,128)} %get-tuple-element.106, pred[512,1024]{1,0:T(8,128)(4,1)S(1)} %copy-done.11, bf16[512,12,64]{0,2,1:T(8,128)(2,1)S(1)} %bitcast.116, bf16[1024,12,64]{0,2,1:T(8,128)(2,1)S(1)} %bitcast.106), kind=kOutput, calls=%fused_computation.4 | convolution fusion | flops 836757504 | bytes 53264384 | tf_op jit(solution)/shard_map/qhd,khd->hqk/dot_general | solution.py:63
  359.0 17.4 %multiply_convert_fusion.1 = bf16[12,512,1024]{2,1,0:T(8,128)(2,1)S(1)} fusion(f32[12,512,1024]{2,1,0:T(8,128)} %get-tuple-element.113, f32[12,512]{1,0:T(8,128)S(1)} %get-tuple-element.112, f32[12,512]{1,0:T(8,128)S(1)} %log_add_fusion.1, f32[12,512,1024]{2,1,0:T(8,128)} %get-tuple-element.106, pred[512,1024]{1,0:T(8,128)(4,1)} %copy.97), kind=kLoop, calls=%fused_computation.3 | loop fusion | flops 37748736 | bytes 63488000 | tf_op jit(solution)/shard_map/convert_element_type | solution.py:65
  389.1 17.8 %multiply_reduce_fusion = (f32[12,512]{1,0:T(8,128)S(1)}, f32[12,512,1024]{2,1,0:T(8,128)}) fusion(f32[12,512]{1,0:T(8,128)S(1)} %log_add_fusion, f32[12,512,1024]{2,1,0:T(8,128)} %get-tuple-element.104, pred[512,1024]{1,0:T(8,128)(4,1)} %copy.100, bf16[512,12,64]{0,2,1:T(8,128)(2,1)} %bitcast.118, bf16[1024,12,64]{0,2,1:T(8,128)(2,1)S(1)} %bitcast.107), kind=kOutput, calls=%fused_computation.1 | convolution fusion | flops 836757504 | bytes 53264384 | tf_op jit(solution)/shard_map/qhd,khd->hqk/dot_general | solution.py:63
  406.9 17.7 %multiply_convert_fusion = bf16[12,512,1024]{2,1,0:T(8,128)(2,1)S(1)} fusion(f32[12,512,1024]{2,1,0:T(8,128)} %get-tuple-element.115, f32[12,512]{1,0:T(8,128)S(1)} %get-tuple-element.114, f32[12,512]{1,0:T(8,128)S(1)} %log_add_fusion, f32[12,512,1024]{2,1,0:T(8,128)} %get-tuple-element.104, pred[512,1024]{1,0:T(8,128)(4,1)} %copy.100), kind=kLoop, calls=%fused_computation | loop fusion | flops 37748736 | bytes 63488000 | tf_op jit(solution)/shard_map/convert_element_type | solution.py:65
  438.5 12.0 %fusion.11 = f32[12,64,1024]{2,1,0:T(8,128)S(1)} fusion(bf16[512,12,64]{0,2,1:T(8,128)(2,1)S(1)} %bitcast.119, f32[12,512]{1,0:T(8,128)S(1)} %log_add_fusion, f32[12,512,1024]{2,1,0:T(8,128)} %get-tuple-element.104, pred[512,1024]{1,0:T(8,128)(4,1)S(1)} %copy-done.14), kind=kOutput, calls=%fused_computation.25 | convolution fusion | flops 830472192 | bytes 29646848 | tf_op jit(solution)/shard_map/hqk,qhd->khd/dot_general | solution.py:73
  450.5 12.1 %convert_reduce_fusion.3 = (f32[12,64]{1,0:T(8,128)S(1)}, bf16[12,64,1024]{2,1,0:T(8,128)(2,1)S(1)}) fusion(f32[12,64,1024]{2,1,0:T(8,128)S(1)} %fusion.11, bf16[512,12,64]{0,2,1:T(8,128)(2,1)S(1)} %bitcast.117, f32[12,512]{1,0:T(8,128)S(1)} %log_add_fusion.1, f32[12,512,1024]{2,1,0:T(8,128)} %get-tuple-element.106, pred[512,1024]{1,0:T(8,128)(4,1)S(1)} %copy-done.12), kind=kOutput, calls=%fused_computation.50 | convolution fusion | flops 833617152 | bytes 31222784 | tf_op jit(solution)/shard_map/hqk,qhd->khd/dot_general | solution.py:73
  463.8 9.1 convolution_bitcast_fusion
  482.8 10.5 fusion.55
  494.7 14.1 %fusion.60 = f32[3072,768]{1,0:T(8,128)} fusion(bf16[1024,768]{0,1:T(8,128)(2,1)S(1)} %copy-done.29, f32[1024,3072]{1,0:T(8,128)} %fusion.57, f32[3072]{0:T(1024)S(1)} %bitcast.135), kind=kOutput, calls=%fused_computation.134 | convolution fusion | flops 4863295488 | bytes 23605248 | tf_op jit(solution)/shard_map/sf,sd->fd/dot_general | solution.py:150
  517.4 90.6 %reduce-scatter.22.cloned.1.call-done = f32[96,2304]{1,0:T(8,128)} async-done(((f32[768,2304]{1,0:T(8,128)}), f32[96,2304]{1,0:T(8,128)}) %reduce-scatter.22.cloned.1.call-update) | async-done | bytes 884752
  610.2 164.4 %reduce-scatter.18.cloned.1.call-done = f32[96,3072]{1,0:T(8,128)} async-done(((f32[768,3072]{1,0:T(8,128)}), f32[96,3072]{1,0:T(8,128)}) %reduce-scatter.18.cloned.1.call-update) | async-done | bytes 1179664 | tf_op jit(solution)/shard_map/reduce_scatter | solution.py:205
  776.7 164.4 %reduce-scatter.20.cloned.1.call-done = f32[384,768]{1,0:T(8,128)} async-done(((f32[3072,768]{1,0:T(8,128)}), f32[384,768]{1,0:T(8,128)}) %reduce-scatter.20.cloned.1.call-update) | async-done | bytes 1179664 | tf_op jit(solution)/shard_map/reduce_scatter | solution.py:206
  943.3 8.9 add_add_fusion.4
  955.8 35.2 %all-reduce = bf16[3072]{0:T(1024)(128)(2,1)S(1)} all-reduce(f32[3072]{0:T(1024)S(1)} %copy-done.43), channel_id=7, replica_groups=mesh['replica'=4,'fsdp'=8] {'fsdp'}, use_global_device_ids=true, to_apply=%region_30.31.clone | all-reduce | flops 3072 | bytes 18432
  991.1 14.3 %reduce-scatter.28.cloned.1.call-done = f32[96,2]{1,0:T(8,128)} async-done(((f32[768,2]{1,0:T(8,128)}), f32[96,2]{1,0:T(8,128)}) %reduce-scatter.28.cloned.1.call-update) | async-done | bytes 784
  1006.2 63.1 %reduce-scatter.26.cloned.1.call-done = f32[96,2]{1,0:T(8,128)} async-done(((f32[768,2]{1,0:T(8,128)}), f32[96,2]{1,0:T(8,128)}) %reduce-scatter.26.cloned.1.call-update) | async-done | bytes 784
  1070.2 63.2 %reduce-scatter.24.cloned.1.call-done = f32[96,4]{1,0:T(8,128)} async-done(((f32[768,4]{1,0:T(8,128)}), f32[96,4]{1,0:T(8,128)}) %reduce-scatter.24.cloned.1.call-update) | async-done | bytes 1552
  1142.2 42.7 %all-reduce.5.cloned.1.call-done = (bf16[96,2304]{0,1:T(8,128)(2,1)}, bf16[96,768]{1,0:T(8,128)(2,1)}, bf16[96,3072]{1,0:T(8,128)(2,1)}, bf16[384,768]{1,0:T(8,128)(2,1)}) async-done(((bf16[96,2304]{0,1:T(8,128)(2,1)}, bf16[96,768]{1,0:T(8,128)(2,1)}, bf16[96,3072]{1,0:T(8,128)(2,1)}, bf16[384,768]{1,0:T(8,128)(2,1)}), (bf16[96,2304]{0,1:T(8,128)(2,1)}, bf16[96,768]{1,0:T(8,128)(2,1)}, ...) | async-done | bytes 1769488 | tf_op jit(solution)/shard_map/psum | solution.py:213
  (231 shorter events, 146.2 us)
Async XLA Ops:
  7.2 99.7 %all-gather.9.cloned.1.call-start = ((), (), s32[]{:S(2)}) async-start(), calls=%async_computation.7 | async-start | bytes 3981312 | tf_op jit(solution)/shard_map/all_gather | solution.py:100
  7.9 192.1 %all-gather.11.cloned.1.call-start = ((), (), s32[]{:S(2)}) async-start(), calls=%async_computation.8 | async-start | bytes 1327104 | tf_op jit(solution)/shard_map/all_gather | solution.py:101
  8.7 195.7 %all-gather.13.cloned.1.call-start = ((), (), s32[]{:S(2)}) async-start(), calls=%async_computation.9 | async-start | bytes 5308416 | tf_op jit(solution)/shard_map/all_gather | solution.py:102
  9.4 92.4 %copy-start.23 = (bf16[1024,768]{1,0:T(8,128)(2,1)S(1)}, bf16[1024,768]{1,0:T(8,128)(2,1)}, u32[]{:S(2)}) copy-start(bf16[1024,768]{1,0:T(8,128)(2,1)} %param.23) | copy-start | bytes 4718596
  9.4 271.8 %all-gather.15.cloned.1.call-start = ((), (), s32[]{:S(2)}) async-start(), calls=%async_computation.10 | async-start | bytes 5308416 | tf_op jit(solution)/shard_map/all_gather | solution.py:103
  10.0 505.8 %reduce-scatter.16.cloned.1.call-start = ((), (), s32[]{:S(2)}) async-start(), calls=%async_computation.11 | async-start | bytes 2654208 | tf_op jit(solution)/shard_map/reduce_scatter | solution.py:204
  106.9 174.3 %copy-start.32 = (f32[768]{0:T(1024)}, f32[768]{0:T(1024)S(1)}, u32[]{:S(2)}) copy-start(f32[768]{0:T(1024)S(1)} %get-tuple-element.71) | copy-start | bytes 9220
  117.3 45.8 %copy-start.2 = (bf16[1024,768]{0,1:T(8,128)(2,1)}, bf16[1024,768]{0,1:T(8,128)(2,1)S(1)}, u32[]{:S(2)}) copy-start(bf16[1024,768]{0,1:T(8,128)(2,1)S(1)} %copy.99) | copy-start | bytes 4718596
  126.5 61.2 %copy-start.7 = (bf16[1024,768]{0,1:T(8,128)(2,1)}, bf16[1024,768]{0,1:T(8,128)(2,1)S(1)}, u32[]{:S(2)}) copy-start(bf16[1024,768]{0,1:T(8,128)(2,1)S(1)} %copy.95) | copy-start | bytes 4718596
  126.5 12.7 %copy-start.13 = (pred[512,1024]{1,0:T(8,128)(4,1)S(1)}, pred[512,1024]{1,0:T(8,128)(4,1)}, u32[]{:S(2)}) copy-start(pred[512,1024]{1,0:T(8,128)(4,1)} %copy.100) | copy-start | bytes 1572868
  139.2 15.5 %copy-start.1 = (f32[12,512,1024]{2,1,0:T(8,128)S(1)}, f32[12,512,1024]{2,1,0:T(8,128)}, u32[]{:S(2)}) copy-start(f32[12,512,1024]{2,1,0:T(8,128)} %get-tuple-element.104) | copy-start | bytes 75497472
  175.3 15.6 %copy-start = (f32[12,512,1024]{2,1,0:T(8,128)S(1)}, f32[12,512,1024]{2,1,0:T(8,128)}, u32[]{:S(2)}) copy-start(f32[12,512,1024]{2,1,0:T(8,128)} %get-tuple-element.106) | copy-start | bytes 75497472
  203.9 124.4 %copy-start.3 = (f32[1024,768]{0,1:T(8,128)}, f32[1024,768]{0,1:T(8,128)S(1)}, u32[]{:S(2)}) copy-start(f32[1024,768]{0,1:T(8,128)S(1)} %get-tuple-element.108) | copy-start | bytes 9437188
  204.4 76.8 %copy-start.44 = (f32[8,1,384]{2,1,0:T(1,128)S(1)}, f32[8,1,384]{2,1,0:T(1,128)}, u32[]{:S(2)}) copy-start(f32[8,1,384]{2,1,0:T(1,128)} %convert_element_type.226) | copy-start | bytes 36868
  204.4 76.8 %copy-start.46 = (f32[768]{0:T(1024)S(1)}, f32[768]{0:T(1024)}, u32[]{:S(2)}) copy-start(f32[768]{0:T(1024)} %get-tuple-element.72) | copy-start | bytes 9220
  296.8 21.6 %slice-start = ((s8[4718592]{0:T(1024)(128)(4,1)}), s8[4194304]{0:T(1024)(128)(4,1)S(1)}, s32[]{:S(2)}) async-start(s8[4718592]{0:T(1024)(128)(4,1)} %bitcast.112), calls=%async_computation.19 | async-start | bytes 8388608
  300.4 18.1 %copy-start.28 = (bf16[1024,768]{0,1:T(8,128)(2,1)}, bf16[1024,768]{0,1:T(8,128)(2,1)S(1)}, u32[]{:S(2)}) copy-start(bf16[1024,768]{0,1:T(8,128)(2,1)S(1)} %get-tuple-element.89) | copy-start | bytes 4718596
  300.4 18.1 %slice-start.1 = ((s8[4718592]{0:T(1024)(128)(4,1)}), s8[524288]{0:T(1024)(128)(4,1)S(1)}, s32[]{:S(2)}) async-start(s8[4718592]{0:T(1024)(128)(4,1)} %bitcast.112), calls=%async_computation.20 | async-start | bytes 1048576
  336.9 22.1 %copy-start.20 = (bf16[512,768]{0,1:T(8,128)(2,1)}, bf16[512,768]{0,1:T(8,128)(2,1)S(1)}, u32[]{:S(2)}) copy-start(bf16[512,768]{0,1:T(8,128)(2,1)S(1)} %get-tuple-element.95) | copy-start | bytes 2359300
  387.7 220.3 %reduce-scatter.22.cloned.1.call-start = ((), (), s32[]{:S(2)}) async-start(), calls=%async_computation.14 | async-start | bytes 7962624
  438.5 12.0 %copy-start.21 = (bf16[512,768]{0,1:T(8,128)(2,1)S(1)}, bf16[512,768]{0,1:T(8,128)(2,1)}, u32[]{:S(2)}) copy-start(bf16[512,768]{0,1:T(8,128)(2,1)} %copy-done.20) | copy-start | bytes 2359300
  450.5 13.3 %copy-start.19 = (bf16[12,64,1024]{2,1,0:T(8,128)(2,1)S(1)}, bf16[12,64,1024]{2,1,0:T(8,128)(2,1)}, u32[]{:S(2)}) copy-start(bf16[12,64,1024]{2,1,0:T(8,128)(2,1)} %multiply_convert_fusion.3) | copy-start | bytes 4718596
  450.5 13.2 %copy-start.25 = (bf16[1024,768]{1,0:T(8,128)(2,1)S(1)}, bf16[1024,768]{1,0:T(8,128)(2,1)}, u32[]{:S(2)}) copy-start(bf16[1024,768]{1,0:T(8,128)(2,1)} %param.12) | copy-start | bytes 4718596
  450.5 13.2 %copy-start.26 = (bf16[1024,12,64]{0,2,1:T(8,128)(2,1)S(1)}, bf16[1024,12,64]{0,2,1:T(8,128)(2,1)}, u32[]{:S(2)}) copy-start(bf16[1024,12,64]{0,2,1:T(8,128)(2,1)} %get-tuple-element.85) | copy-start | bytes 4718596
  480.9 293.7 %reduce-scatter.18.cloned.1.call-start = ((), (), s32[]{:S(2)}) async-start(), calls=%async_computation.12 | async-start | bytes 10616832 | tf_op jit(solution)/shard_map/reduce_scatter | solution.py:205
  493.3 447.9 %reduce-scatter.20.cloned.1.call-start = ((), (), s32[]{:S(2)}) async-start(), calls=%async_computation.13 | async-start | bytes 10616832 | tf_op jit(solution)/shard_map/reduce_scatter | solution.py:206
  508.9 496.5 %reduce-scatter.28.cloned.1.call-start = ((), (), s32[]{:S(2)}) async-start(), calls=%async_computation.17 | async-start | bytes 442368
  510.5 558.7 %reduce-scatter.26.cloned.1.call-start = ((), (), s32[]{:S(2)}) async-start(), calls=%async_computation.16 | async-start | bytes 442368
  511.8 621.6 %reduce-scatter.24.cloned.1.call-start = ((), (), s32[]{:S(2)}) async-start(), calls=%async_computation.15 | async-start | bytes 442368
  512.9 672.1 %all-reduce.5.cloned.1.call-start = ((), (), s32[]{:S(2)}) async-start(), calls=%async_computation.18 | async-start | bytes 3833856 | tf_op jit(solution)/shard_map/psum | solution.py:213
  517.4 425.9 %copy-start.16 = (f32[1024,768]{0,1:T(8,128)S(1)}, f32[1024,768]{0,1:T(8,128)}, u32[]{:S(2)}) copy-start(f32[1024,768]{0,1:T(8,128)} %copy-done.15) | copy-start | bytes 9437188
  517.4 426.0 %copy-start.41 = (f32[1024]{0:T(1024)S(1)}, f32[1024]{0:T(1024)}, u32[]{:S(2)}) copy-start(f32[1024]{0:T(1024)} %copy-done.40) | copy-start | bytes 12292
  (34 other events, 136.6 us)
Sparse Core Ops, SparseCore 0:
  10.2 68.0 all-gather.8
  80.5 39.7 all-gather.10
  122.4 78.6 all-gather.12
  203.1 78.0 all-gather.14
  387.8 67.3 reduce-scatter.15
  481.0 126.8 reduce-scatter.21
  612.0 162.5 reduce-scatter.17
  778.6 162.5 reduce-scatter.19
  944.8 60.5 reduce-scatter.27
  1008.8 60.4 reduce-scatter.25
  1072.9 60.4 reduce-scatter.23
  1136.6 48.2 all-reduce.4
where the time goes:
time: 1210 us; the launch traced here: 1200 us
  waiting for transfers between devices  671 us (55%)
  matrix products  234 us (19%)
  blocking collectives  124 us (10%)
  other arithmetic  94.4 us (8%)
  local copies, waits for them, and re-layouts  59 us (5%)
  between operations  16.3 us (1%)
    unnamed x16, waiting for transfers between devices  234 us
    reduce_scatter x1, waiting for transfers between devices, shards(): lax.psum_scatter(down_grad, 'fsdp', scatter_dimension=0, tiled=True)  164 us
    reduce_scatter x1, waiting for transfers between devices, shards(): lax.psum_scatter(up_grad, 'fsdp', scatter_dimension=0, tiled=True)  164 us
    all_gather x1, waiting for transfers between devices, shards(): lax.all_gather(down_weight, 'fsdp', axis=0, tiled=True)  65.6 us
    unnamed x126, local copies, waits for them, and re-layouts  48.3 us
    psum x1, waiting for transfers between devices, shards(): lax.psum(as_sent(tuple(shares)), 'replica')  42.7 us
    dot_general x2, matrix products, backward_block(): jnp.einsum('qhd,khd->hqk', grad_block, values, preferred_element_type=jnp...  39.2 us
    unnamed x1, blocking collectives  35.2 us
  transfers between devices with their start and end apart: 12, of which 8 were waited for; matrix products, arithmetic and copies ran while one was open for 21% of the time, Pallas kernels for 0%

commit v1 on v0

--- a/solution.py
+++ b/solution.py
@@ -9,6 +9,19 @@
 HD = 64
 BLK = 64
 norm_eps = 1e-06
+
+
+def collect(shard, axis, dim):
+    ways = lax.axis_size(axis)
+    up = [(d, (d + 1) % ways) for d in range(ways)]
+    down = [(d, (d - 1) % ways) for d in range(ways)]
+    earlier, later = ([shard], [shard])
+    for _ in range(ways // 2):
+        earlier.append(lax.ppermute(earlier[-1], axis, up))
+    for _ in range((ways - 1) // 2):
+        later.append(lax.ppermute(later[-1], axis, down))
+    line = jnp.concatenate([*earlier[::-1], *later[1:]], axis=dim)
+    return jnp.roll(line, (lax.axis_index(axis) - ways // 2) * shard.shape[dim], axis=dim)
 
 
 def as_sent(array):
@@ -102,7 +115,7 @@
         lax.all_gather(up_weight, "fsdp", axis=0, tiled=True),
         lax.all_gather(down_weight, "fsdp", axis=0, tiled=True),
         lax.all_gather(proj_bias, "fsdp", axis=1, tiled=True),
-        lax.all_gather(up_bias, "fsdp", axis=0, tiled=True),
+        collect(up_bias, "fsdp", 0),
         lax.all_gather(norm_gain, "fsdp", axis=1, tiled=True),
         lax.all_gather(norm_bias, "fsdp", axis=1, tiled=True),
     )

time: 1210 us -> 1200 us (level)
  blocking collectives: 124 us -> 94.3 us
  starting transfers between devices: 0.48 us -> 16.2 us
    all_gather x1 -> x0, blocking collectives: 25.9 us -> none  [shards(): lax.all_gather(up_bias, 'fsdp', axis=0, tiled=True)]
    ppermute x0 -> x7, starting transfers between devices: none -> 15.7 us  [the longest x3 12.7 us: collect(): later.append(lax.ppermute(later[-1], axis, down))]
    unnamed x126 -> x144, local copies, waits for them, and re-layouts: 48.3 us -> 50.3 us
  transfers between devices with their start and end apart: 12 -> 19, of which waited for: 8 -> 11; matrix products, arithmetic and copies ran while one was open for 21% -> 22% of each run, Pallas kernels for 0% -> 0%
where the time goes in v1:
time: 1200 us
  waiting for transfers between devices  683 us (57%)
  matrix products  233 us (19%)
  other arithmetic  94.5 us (8%)
  blocking collectives  94.3 us (8%)
  local copies, waits for them, and re-layouts  61.2 us (5%)
  between operations  16.4 us (1%)
  starting transfers between devices  16.2 us (1%)
    unnamed x16, waiting for transfers between devices  234 us
    reduce_scatter x1, waiting for transfers between devices, shards(): lax.psum_scatter(down_grad, 'fsdp', scatter_dimension=0, tiled=True)  164 us
    reduce_scatter x1, waiting for transfers between devices, shards(): lax.psum_scatter(up_grad, 'fsdp', scatter_dimension=0, tiled=True)  164 us
    all_gather x1, waiting for transfers between devices, shards(): lax.all_gather(down_weight, 'fsdp', axis=0, tiled=True)  69.1 us
    unnamed x144, local copies, waits for them, and re-layouts  50.3 us
    psum x1, waiting for transfers between devices, shards(): lax.psum(as_sent(tuple(shares)), 'replica')  42.6 us
    dot_general x2, matrix products, backward_block(): jnp.einsum('qhd,khd->hqk', grad_block, values, preferred_element_type=jnp...  39.8 us
    unnamed x1, blocking collectives  35.2 us
  transfers between devices with their start and end apart: 19, of which 11 were waited for; matrix products, arithmetic and copies ran while one was open for 22% of the time, Pallas kernels for 0%

profile of v1, /device:TPU:0, one launch (start us, length us, event | category | flops | bytes accessed | tf_op | source)
XLA Modules:
  0.0 1198.8 jit_solution(7749272504422463578)
XLA Ops:
  17.3 18.3 %all-gather.1 = bf16[8,96,2]{1,2,0:T(2,128)(2,1)S(1)} all-gather(bf16[1,96,2]{1,2,0:T(2,128)(2,1)} %bitcast.134), channel_id=1, replica_groups=mesh['replica'=4,'fsdp'=8] {'fsdp'}, dimensions={0}, use_global_device_ids=true | all-gather | bytes 3456 | tf_op jit(solution)/shard_map/all_gather | solution.py:119
  35.6 16.6 %all-gather.2 = bf16[8,96,2]{1,2,0:T(2,128)(2,1)S(1)} all-gather(bf16[1,96,2]{1,2,0:T(2,128)(2,1)} %bitcast.135), channel_id=1, replica_groups=mesh['replica'=4,'fsdp'=8] {'fsdp'}, dimensions={0}, use_global_device_ids=true | all-gather | bytes 3456 | tf_op jit(solution)/shard_map/all_gather | solution.py:120
  52.3 18.6 %all-gather = bf16[8,96,4]{1,2,0:T(4,128)(2,1)S(1)} all-gather(bf16[1,96,4]{1,2,0:T(4,128)(2,1)} %bitcast.133), channel_id=1, replica_groups=mesh['replica'=4,'fsdp'=8] {'fsdp'}, dimensions={0}, use_global_device_ids=true | all-gather | bytes 6912 | tf_op jit(solution)/shard_map/all_gather | solution.py:117
  121.7 12.9 %fusion.20 = (f32[12,512]{1,0:T(8,128)S(1)}, f32[12,512,1024]{2,1,0:T(8,128)}) fusion(pred[512,1024]{1,0:T(8,128)(4,1)} %copy.100, bf16[512,12,64]{0,2,1:T(8,128)(2,1)} %bitcast.107, bf16[1024,12,64]{0,2,1:T(8,128)(2,1)S(1)} %bitcast.99), kind=kOutput, calls=%fused_computation.34 | convolution fusion | flops 824174592 | bytes 28073984 | tf_op jit(solution)/shard_map/qhd,khd->hqk/dot_general | solution.py:58
  134.6 12.7 %fusion.1 = f32[12,512]{1,0:T(8,128)S(1)} fusion(f32[12,512]{1,0:T(8,128)S(1)} %get-tuple-element.103, f32[12,512,1024]{2,1,0:T(8,128)} %get-tuple-element.104, pred[512,1024]{1,0:T(8,128)(4,1)S(1)} %copy-done.13), kind=kLoop, calls=%fused_computation.13 | loop fusion | flops 25159680 | bytes 25739264 | tf_op jit(solution)/shard_map/reduce_sum | solution.py:67
  150.2 8.4 fusion.32
  158.7 12.0 %fusion.19 = (f32[12,512]{1,0:T(8,128)S(1)}, f32[12,512,1024]{2,1,0:T(8,128)}) fusion(pred[512,1024]{1,0:T(8,128)(4,1)S(1)} %copy-done.10, bf16[512,12,64]{0,2,1:T(8,128)(2,1)} %bitcast.109, bf16[1024,12,64]{0,2,1:T(8,128)(2,1)S(1)} %bitcast.100), kind=kOutput, calls=%fused_computation.33 | convolution fusion | flops 824174592 | bytes 28073984 | tf_op jit(solution)/shard_map/qhd,khd->hqk/dot_general | solution.py:58
  170.7 12.3 %fusion = f32[12,512]{1,0:T(8,128)S(1)} fusion(f32[12,512]{1,0:T(8,128)S(1)} %get-tuple-element.105, f32[12,512,1024]{2,1,0:T(8,128)} %get-tuple-element.106, pred[512,1024]{1,0:T(8,128)(4,1)S(1)} %copy-done.10), kind=kLoop, calls=%fused_computation.12 | loop fusion | flops 25159680 | bytes 25739264 | tf_op jit(solution)/shard_map/reduce_sum | solution.py:67
  201.3 11.0 fusion.57
  212.3 69.1 %all-gather.14.cloned.1.call-done = bf16[3072,768]{1,0:T(8,128)(2,1)} async-done(((bf16[384,768]{1,0:T(8,128)(2,1)}), bf16[3072,768]{1,0:T(8,128)(2,1)}) %all-gather.14.cloned.1.call-update) | async-done | bytes 4718608 | tf_op jit(solution)/shard_map/all_gather | solution.py:116
  281.4 11.5 fusion.66
  300.3 18.2 %convert_reduce_fusion = (f32[3072]{0:T(1024)}, bf16[1024,3072]{1,0:T(8,128)(2,1)}) fusion(f32[1024,3072]{1,0:T(8,128)} %fusion.57, f32[3072]{0:T(1024)S(1)} %copy-done.45, bf16[1024,768]{0,1:T(8,128)(2,1)S(1)} %get-tuple-element.89, bf16[3072,768]{1,0:T(8,128)(2,1)} %all-gather.14.cloned.1.call-done), kind=kOutput, calls=%fused_computation.27 | convolution fusion | flops 4904186880 | bytes 25190400 | tf_op jit(solution)/shard_map/sd,fd->sf/dot_general | solution.py:166
  318.5 9.4 multiply_reduce_fusion.3
  337.3 21.5 %multiply_reduce_fusion.1 = (f32[12,512]{1,0:T(8,128)S(1)}, f32[12,512,1024]{2,1,0:T(8,128)}) fusion(f32[12,512]{1,0:T(8,128)S(1)} %log_add_fusion.1, f32[12,512,1024]{2,1,0:T(8,128)} %get-tuple-element.106, pred[512,1024]{1,0:T(8,128)(4,1)S(1)} %copy-done.11, bf16[512,12,64]{0,2,1:T(8,128)(2,1)S(1)} %bitcast.115, bf16[1024,12,64]{0,2,1:T(8,128)(2,1)S(1)} %bitcast.105), kind=kOutput, calls=%fused_computation.4 | convolution fusion | flops 836757504 | bytes 53264384 | tf_op jit(solution)/shard_map/qhd,khd->hqk/dot_general | solution.py:76
  358.8 17.2 %multiply_convert_fusion.1 = bf16[12,512,1024]{2,1,0:T(8,128)(2,1)S(1)} fusion(f32[12,512,1024]{2,1,0:T(8,128)} %get-tuple-element.113, f32[12,512]{1,0:T(8,128)S(1)} %get-tuple-element.112, f32[12,512]{1,0:T(8,128)S(1)} %log_add_fusion.1, f32[12,512,1024]{2,1,0:T(8,128)} %get-tuple-element.106, pred[512,1024]{1,0:T(8,128)(4,1)} %copy.97), kind=kLoop, calls=%fused_computation.3 | loop fusion | flops 37748736 | bytes 63488000 | tf_op jit(solution)/shard_map/convert_element_type | solution.py:78
  388.7 18.2 %multiply_reduce_fusion = (f32[12,512]{1,0:T(8,128)S(1)}, f32[12,512,1024]{2,1,0:T(8,128)}) fusion(f32[12,512]{1,0:T(8,128)S(1)} %log_add_fusion, f32[12,512,1024]{2,1,0:T(8,128)} %get-tuple-element.104, pred[512,1024]{1,0:T(8,128)(4,1)} %copy.100, bf16[512,12,64]{0,2,1:T(8,128)(2,1)} %bitcast.117, bf16[1024,12,64]{0,2,1:T(8,128)(2,1)S(1)} %bitcast.106), kind=kOutput, calls=%fused_computation.1 | convolution fusion | flops 836757504 | bytes 53264384 | tf_op jit(solution)/shard_map/qhd,khd->hqk/dot_general | solution.py:76
  407.0 17.6 %multiply_convert_fusion = bf16[12,512,1024]{2,1,0:T(8,128)(2,1)S(1)} fusion(f32[12,512,1024]{2,1,0:T(8,128)} %get-tuple-element.115, f32[12,512]{1,0:T(8,128)S(1)} %get-tuple-element.114, f32[12,512]{1,0:T(8,128)S(1)} %log_add_fusion, f32[12,512,1024]{2,1,0:T(8,128)} %get-tuple-element.104, pred[512,1024]{1,0:T(8,128)(4,1)} %copy.100), kind=kLoop, calls=%fused_computation | loop fusion | flops 37748736 | bytes 63488000 | tf_op jit(solution)/shard_map/convert_element_type | solution.py:78
  438.5 11.9 fusion.11
  450.5 12.1 %convert_reduce_fusion.3 = (f32[12,64]{1,0:T(8,128)S(1)}, bf16[12,64,1024]{2,1,0:T(8,128)(2,1)S(1)}) fusion(f32[12,64,1024]{2,1,0:T(8,128)S(1)} %fusion.11, bf16[512,12,64]{0,2,1:T(8,128)(2,1)S(1)} %bitcast.116, f32[12,512]{1,0:T(8,128)S(1)} %log_add_fusion.1, f32[12,512,1024]{2,1,0:T(8,128)} %get-tuple-element.106, pred[512,1024]{1,0:T(8,128)(4,1)S(1)} %copy-done.12), kind=kOutput, calls=%fused_computation.50 | convolution fusion | flops 833617152 | bytes 31222784 | tf_op jit(solution)/shard_map/hqk,qhd->khd/dot_general | solution.py:86
  463.7 9.1 convolution_bitcast_fusion
  472.9 8.0 copy.112
  482.8 10.5 fusion.55
  494.7 13.9 %fusion.60 = f32[3072,768]{1,0:T(8,128)} fusion(bf16[1024,768]{0,1:T(8,128)(2,1)S(1)} %copy-done.29, f32[1024,3072]{1,0:T(8,128)} %fusion.57, f32[3072]{0:T(1024)S(1)} %copy-done.46), kind=kOutput, calls=%fused_computation.135 | convolution fusion | flops 4863295488 | bytes 23605248 | tf_op jit(solution)/shard_map/sf,sd->fd/dot_general | solution.py:163
  517.1 90.9 %reduce-scatter.22.cloned.1.call-done = f32[96,2304]{1,0:T(8,128)} async-done(((f32[768,2304]{1,0:T(8,128)}), f32[96,2304]{1,0:T(8,128)}) %reduce-scatter.22.cloned.1.call-update) | async-done | bytes 884752
  610.2 164.2 %reduce-scatter.18.cloned.1.call-done = f32[96,3072]{1,0:T(8,128)} async-done(((f32[768,3072]{1,0:T(8,128)}), f32[96,3072]{1,0:T(8,128)}) %reduce-scatter.18.cloned.1.call-update) | async-done | bytes 1179664 | tf_op jit(solution)/shard_map/reduce_scatter | solution.py:218
  776.6 164.3 %reduce-scatter.20.cloned.1.call-done = f32[384,768]{1,0:T(8,128)} async-done(((f32[3072,768]{1,0:T(8,128)}), f32[384,768]{1,0:T(8,128)}) %reduce-scatter.20.cloned.1.call-update) | async-done | bytes 1179664 | tf_op jit(solution)/shard_map/reduce_scatter | solution.py:219
  943.1 8.9 add_add_fusion.4
  955.5 35.2 %all-reduce = bf16[3072]{0:T(1024)(128)(2,1)S(1)} all-reduce(f32[3072]{0:T(1024)S(1)} %copy-done.44), channel_id=7, replica_groups=mesh['replica'=4,'fsdp'=8] {'fsdp'}, use_global_device_ids=true, to_apply=%region_30.31.clone | all-reduce | flops 3072 | bytes 18432
  990.8 14.3 %reduce-scatter.28.cloned.1.call-done = f32[96,2]{1,0:T(8,128)} async-done(((f32[768,2]{1,0:T(8,128)}), f32[96,2]{1,0:T(8,128)}) %reduce-scatter.28.cloned.1.call-update) | async-done | bytes 784
  1006.0 63.1 %reduce-scatter.26.cloned.1.call-done = f32[96,2]{1,0:T(8,128)} async-done(((f32[768,2]{1,0:T(8,128)}), f32[96,2]{1,0:T(8,128)}) %reduce-scatter.26.cloned.1.call-update) | async-done | bytes 784
  1069.9 63.2 %reduce-scatter.24.cloned.1.call-done = f32[96,4]{1,0:T(8,128)} async-done(((f32[768,4]{1,0:T(8,128)}), f32[96,4]{1,0:T(8,128)}) %reduce-scatter.24.cloned.1.call-update) | async-done | bytes 1552
  1141.9 42.6 %all-reduce.5.cloned.1.call-done = (bf16[96,2304]{0,1:T(8,128)(2,1)}, bf16[96,768]{1,0:T(8,128)(2,1)}, bf16[96,3072]{1,0:T(8,128)(2,1)}, bf16[384,768]{1,0:T(8,128)(2,1)}) async-done(((bf16[96,2304]{0,1:T(8,128)(2,1)}, bf16[96,768]{1,0:T(8,128)(2,1)}, bf16[96,3072]{1,0:T(8,128)(2,1)}, bf16[384,768]{1,0:T(8,128)(2,1)}), (bf16[96,2304]{0,1:T(8,128)(2,1)}, bf16[96,768]{1,0:T(8,128)(2,1)}, ...) | async-done | bytes 1769488 | tf_op jit(solution)/shard_map/psum | solution.py:226
  (264 shorter events, 164.6 us)
Async XLA Ops:
  7.2 94.9 %all-gather.8.cloned.1.call-start = ((), (), s32[]{:S(2)}) async-start(), calls=%async_computation.7 | async-start | bytes 3981312 | tf_op jit(solution)/shard_map/all_gather | solution.py:113
  7.9 187.4 %all-gather.10.cloned.1.call-start = ((), (), s32[]{:S(2)}) async-start(), calls=%async_computation.8 | async-start | bytes 1327104 | tf_op jit(solution)/shard_map/all_gather | solution.py:114
  8.7 192.6 %all-gather.12.cloned.1.call-start = ((), (), s32[]{:S(2)}) async-start(), calls=%async_computation.9 | async-start | bytes 5308416 | tf_op jit(solution)/shard_map/all_gather | solution.py:115
  9.4 79.5 %copy-start.23 = (bf16[1024,768]{1,0:T(8,128)(2,1)S(1)}, bf16[1024,768]{1,0:T(8,128)(2,1)}, u32[]{:S(2)}) copy-start(bf16[1024,768]{1,0:T(8,128)(2,1)} %param.23) | copy-start | bytes 4718596
  9.4 271.9 %all-gather.14.cloned.1.call-start = ((), (), s32[]{:S(2)}) async-start(), calls=%async_computation.10 | async-start | bytes 5308416 | tf_op jit(solution)/shard_map/all_gather | solution.py:116
  9.5 63.9 %collective-permute-start = (bf16[384]{0:T(512)(128)(2,1)}, bf16[384]{0:T(512)(128)(2,1)S(1)}, u32[]{:S(2)}, u32[]{:S(2)}) collective-permute-start(bf16[384]{0:T(512)(128)(2,1)} %param.20), channel_id=1, source_target_pairs={{0,1},{1,2},{2,3},{3,4},{4,5},{5,6},{6,7},{7,0},{8,9},{9,10},{10,1... | collective-permute-start | bytes 2312 | tf_op jit(solution)/shard_map/ppermute | solution.py:20
  12.5 67.2 %collective-permute-start.4 = (bf16[384]{0:T(512)(128)(2,1)}, bf16[384]{0:T(512)(128)(2,1)S(1)}, u32[]{:S(2)}, u32[]{:S(2)}) collective-permute-start(bf16[384]{0:T(512)(128)(2,1)} %param.20), channel_id=1, source_target_pairs={{0,7},{1,0},{2,1},{3,2},{4,3},{5,4},{6,5},{7,6},{8,15},{9,8},{10,9... | collective-permute-start | bytes 2312 | tf_op jit(solution)/shard_map/ppermute | solution.py:22
  15.6 499.9 %reduce-scatter.16.cloned.1.call-start = ((), (), s32[]{:S(2)}) async-start(), calls=%async_computation.11 | async-start | bytes 2654208 | tf_op jit(solution)/shard_map/reduce_scatter | solution.py:217
  73.4 6.3 collective-permute-start.1
  79.7 6.3 collective-permute-start.2
  79.7 13.6 %collective-permute-start.5 = (bf16[384]{0:T(512)(128)(2,1)S(1)}, bf16[384]{0:T(512)(128)(2,1)S(1)}, u32[]{:S(2)}, u32[]{:S(2)}) collective-permute-start(bf16[384]{0:T(512)(128)(2,1)S(1)} %collective-permute-done.4), channel_id=1, source_target_pairs={{0,7},{1,0},{2,1},{3,2},{4,3},{5,4},{6,5},{7,6},{8,15},{9,8},{10,9... | collective-permute-start | bytes 2312 | tf_op jit(solution)/shard_map/ppermute | solution.py:22
  85.9 12.2 %collective-permute-start.3 = (bf16[384]{0:T(512)(128)(2,1)S(1)}, bf16[384]{0:T(512)(128)(2,1)S(1)}, u32[]{:S(2)}, u32[]{:S(2)}) collective-permute-start(bf16[384]{0:T(512)(128)(2,1)S(1)} %collective-permute-done.2), channel_id=1, source_target_pairs={{0,1},{1,2},{2,3},{3,4},{4,5},{5,6},{6,7},{7,0},{8,9},{9,10},{10,1... | collective-permute-start | bytes 2312 | tf_op jit(solution)/shard_map/ppermute | solution.py:20
  93.2 6.3 collective-permute-start.6
  112.5 46.2 %copy-start.2 = (bf16[1024,768]{0,1:T(8,128)(2,1)}, bf16[1024,768]{0,1:T(8,128)(2,1)S(1)}, u32[]{:S(2)}) copy-start(bf16[1024,768]{0,1:T(8,128)(2,1)S(1)} %copy.99) | copy-start | bytes 4718596
  121.7 61.3 %copy-start.7 = (bf16[1024,768]{0,1:T(8,128)(2,1)}, bf16[1024,768]{0,1:T(8,128)(2,1)S(1)}, u32[]{:S(2)}) copy-start(bf16[1024,768]{0,1:T(8,128)(2,1)S(1)} %copy.95) | copy-start | bytes 4718596
  134.6 15.6 %copy-start.1 = (f32[12,512,1024]{2,1,0:T(8,128)S(1)}, f32[12,512,1024]{2,1,0:T(8,128)}, u32[]{:S(2)}) copy-start(f32[12,512,1024]{2,1,0:T(8,128)} %get-tuple-element.104) | copy-start | bytes 75497472
  199.1 128.8 %copy-start.3 = (f32[1024,768]{0,1:T(8,128)}, f32[1024,768]{0,1:T(8,128)S(1)}, u32[]{:S(2)}) copy-start(f32[1024,768]{0,1:T(8,128)S(1)} %get-tuple-element.108) | copy-start | bytes 9437188
  201.3 80.1 %copy-start.45 = (f32[3072]{0:T(1024)S(1)}, f32[3072]{0:T(1024)}, u32[]{:S(2)}) copy-start(f32[3072]{0:T(1024)} %dynamic-slice_convert_fusion) | copy-start | bytes 36868
  201.3 80.1 %copy-start.47 = (f32[768]{0:T(1024)S(1)}, f32[768]{0:T(1024)}, u32[]{:S(2)}) copy-start(f32[768]{0:T(1024)} %get-tuple-element.72) | copy-start | bytes 9220
  296.7 21.8 %slice-start = ((s8[4718592]{0:T(1024)(128)(4,1)}), s8[4194304]{0:T(1024)(128)(4,1)S(1)}, s32[]{:S(2)}) async-start(s8[4718592]{0:T(1024)(128)(4,1)} %bitcast.111), calls=%async_computation.19 | async-start | bytes 8388608
  300.3 18.2 %copy-start.28 = (bf16[1024,768]{0,1:T(8,128)(2,1)}, bf16[1024,768]{0,1:T(8,128)(2,1)S(1)}, u32[]{:S(2)}) copy-start(bf16[1024,768]{0,1:T(8,128)(2,1)S(1)} %get-tuple-element.89) | copy-start | bytes 4718596
  300.3 18.2 %slice-start.1 = ((s8[4718592]{0:T(1024)(128)(4,1)}), s8[524288]{0:T(1024)(128)(4,1)S(1)}, s32[]{:S(2)}) async-start(s8[4718592]{0:T(1024)(128)(4,1)} %bitcast.111), calls=%async_computation.20 | async-start | bytes 1048576
  336.5 22.3 %copy-start.20 = (bf16[512,768]{0,1:T(8,128)(2,1)}, bf16[512,768]{0,1:T(8,128)(2,1)S(1)}, u32[]{:S(2)}) copy-start(bf16[512,768]{0,1:T(8,128)(2,1)S(1)} %get-tuple-element.95) | copy-start | bytes 2359300
  387.4 220.7 %reduce-scatter.22.cloned.1.call-start = ((), (), s32[]{:S(2)}) async-start(), calls=%async_computation.14 | async-start | bytes 7962624
  480.9 293.5 %reduce-scatter.18.cloned.1.call-start = ((), (), s32[]{:S(2)}) async-start(), calls=%async_computation.12 | async-start | bytes 10616832 | tf_op jit(solution)/shard_map/reduce_scatter | solution.py:218
  493.3 447.6 %reduce-scatter.20.cloned.1.call-start = ((), (), s32[]{:S(2)}) async-start(), calls=%async_computation.13 | async-start | bytes 10616832 | tf_op jit(solution)/shard_map/reduce_scatter | solution.py:219
  508.7 496.4 %reduce-scatter.28.cloned.1.call-start = ((), (), s32[]{:S(2)}) async-start(), calls=%async_computation.17 | async-start | bytes 442368
  510.3 558.7 %reduce-scatter.26.cloned.1.call-start = ((), (), s32[]{:S(2)}) async-start(), calls=%async_computation.16 | async-start | bytes 442368
  511.5 621.6 %reduce-scatter.24.cloned.1.call-start = ((), (), s32[]{:S(2)}) async-start(), calls=%async_computation.15 | async-start | bytes 442368
  512.6 672.0 %all-reduce.5.cloned.1.call-start = ((), (), s32[]{:S(2)}) async-start(), calls=%async_computation.18 | async-start | bytes 3833856 | tf_op jit(solution)/shard_map/psum | solution.py:226
  517.1 425.9 %copy-start.16 = (f32[1024,768]{0,1:T(8,128)S(1)}, f32[1024,768]{0,1:T(8,128)}, u32[]{:S(2)}) copy-start(f32[1024,768]{0,1:T(8,128)} %copy-done.15) | copy-start | bytes 9437188
  517.1 426.0 %copy-start.42 = (f32[1024]{0:T(1024)S(1)}, f32[1024]{0:T(1024)}, u32[]{:S(2)}) copy-start(f32[1024]{0:T(1024)} %copy-done.41) | copy-start | bytes 12292
  (43 other events, 238.2 us)
Sparse Core Ops, SparseCore 0:
  10.2 68.0 all-gather.7
  80.4 39.7 all-gather.9
  122.4 78.7 all-gather.11
  203.3 78.0 all-gather.13
  387.5 67.2 reduce-scatter.15
  481.0 126.9 reduce-scatter.21
  612.0 162.3 reduce-scatter.17
  778.4 162.4 reduce-scatter.19
  944.5 60.5 reduce-scatter.27
  1008.6 60.4 reduce-scatter.25
  1072.6 60.4 reduce-scatter.23
  1136.4 48.1 all-reduce.4
